TPU v7x, 32 devices: a whole 2x2x4 slice. The times are simulated.
32 devices in a mesh: groups: 2 (over y), tmpl: 16 (over z, x, core).
Axes of the slice: x: 2, y: 2, z: 4, core: 2. Of those that a mesh axis runs over, the one named last changes fastest.
Arguments:
- records: bfloat16 [512, 3, 768], P(('groups', 'tmpl')), parts along dimension 0, may hold values from -200 to 200, as said below
- templates: bfloat16 [96, 20, 3, 300], P('tmpl'), may hold values from -6 to 6
- fetch_list: int32 [16, 16, 2], P('tmpl'), may hold values from -1 to 15, as said below
- cluster_slots: int32 [96, 20], P('tmpl'), may hold values from 0 to 31, as said below
- moveouts: int32 [96, 20], P('tmpl'), may hold values from 0 to 213
Outputs:
- stack: float32 [192, 256], P(('groups', 'tmpl')), parts along dimension 0
- network_peak: float32 [512], P('groups'), parts along dimension 0
There are 2 independent parts, one for each index of `groups`. A program takes and returns all parts, laid end to end along the dimension named above; an argument that names none is the same for every part. Nothing has to cross between parts.
Inputs may be any that keep to these rules, and one draw needn't show every extreme that they name: Values are the records' samples; the amplitude of a station component is steady apart from one event burst. fetch_list[g, o, s] is an index among holder o's 16 stations, or -1 for an empty slot; the set entries of one (g, o) pair differ; every group g has all 2 slots set for the holders g to g + 20 // 2 - 1 (modulo 16). cluster_slots[k, j] is a slot o * 2 + s of group k // 6 whose fetch_list entry is set; the 20 entries of a station set differ, and every set slot of a group is named by some station set of that group.
All inputs are finite; a program needn't handle non-finite values.
Results may differ from a plain program's by a relative error of at most 0.0003.
Values may be sent and summed in bfloat16 or wider, within the bound.
A program may use at most 64 MiB of HBM per device.

v0:
```python
import jax
import jax.numpy as jnp
from jax import lax
from jax.sharding import PartitionSpec as P

OUT = 256


def batch_stack(traces, kernels, shifts):
    sets_here, stations, comps, rec_len = traces.shape
    members = kernels.shape[1]
    tap_count = kernels.shape[-1]
    lag_count = rec_len - tap_count + 1
    inputs_nch = traces.reshape(1, sets_here * stations * comps, rec_len)
    filters = jnp.transpose(kernels, (0, 2, 3, 1, 4)).reshape(
        sets_here * stations * comps * members, 1, tap_count
    )
    products = lax.conv_general_dilated(
        inputs_nch,
        filters,
        (1,),
        "VALID",
        dimension_numbers=("NCH", "OIH", "NCH"),
        feature_group_count=sets_here * stations * comps,
        preferred_element_type=jnp.float32,
    )[0]
    products = products.reshape(sets_here, stations, comps, members, lag_count)
    widened = traces.astype(jnp.float32)
    running = jnp.cumsum(widened * widened, axis=-1)
    running = jnp.concatenate(
        [jnp.zeros((sets_here, stations, comps, 1), jnp.float32), running], axis=-1
    )
    energy = running[..., tap_count:] - running[..., :lag_count]
    data_scale = jnp.sqrt(energy / tap_count + 1e-05)
    kernels_wide = kernels.astype(jnp.float32)
    tmpl_scale = jnp.sqrt(jnp.mean(kernels_wide * kernels_wide, axis=-1) + 1e-05)
    tmpl_scale = jnp.transpose(tmpl_scale, (0, 2, 3, 1))[..., None]
    normed = products / (tap_count * tmpl_scale * data_scale[:, :, :, None, :])
    channel_sum = jnp.sum(normed, axis=2)
    offsets = jnp.transpose(shifts, (0, 2, 1))[..., None] + jnp.arange(OUT, dtype=jnp.int32)
    aligned = jnp.take_along_axis(channel_sum, offsets, axis=3)
    return jnp.sum(aligned, axis=1)


def on_device(records, templates, fetch_list, cluster_slots, moveouts):
    owners = lax.axis_size("tmpl")
    per_owner = fetch_list.shape[2]
    stations_here = records.shape[0]
    slot_total = owners * per_owner
    wanted = fetch_list.reshape(slot_total)
    block_rows = lax.all_gather(records, "tmpl", axis=0, tiled=True)
    owners_in = block_rows.shape[0] // stations_here
    row_ids = jnp.arange(
        owners_in * per_owner, dtype=jnp.int32
    ) // per_owner * stations_here + jnp.clip(wanted, 0, stations_here - 1)
    rows_taken = jnp.take(block_rows, row_ids, axis=0)
    rows_taken = jnp.where(
        (wanted >= 0)[:, None, None], rows_taken, jnp.zeros((), block_rows.dtype)
    )
    clusters_here = cluster_slots.shape[0]
    members = templates.shape[0] // clusters_here
    kernels_all = templates.reshape((clusters_here, members) + templates.shape[1:])
    shifts_all = moveouts.reshape(clusters_here, members, moveouts.shape[1])
    traces = jnp.take(rows_taken, cluster_slots, axis=0)
    stacks = batch_stack(traces, kernels_all, shifts_all)
    stack = stacks.reshape(clusters_here * members, stacks.shape[-1])
    network_peak = lax.pmax(jnp.max(stack, axis=0), "tmpl")
    return (stack, network_peak)


def solution(mesh):
    placed = (
        P(("groups", "tmpl"), None, None),
        P("tmpl", None, None, None),
        P("tmpl", None, None),
        P("tmpl", None),
        P("tmpl", None),
    )
    return jax.shard_map(
        on_device,
        mesh=mesh,
        in_specs=placed,
        out_specs=(P(("groups", "tmpl"), None), P("groups")),
        check_vma=False,
    )
```

profile of v0, /device:TPU:0, one launch (start us, length us, event | category | flops | bytes accessed | tf_op | source)
XLA Modules:
  0.0 464.8 jit_solution(15089831089222544754)
XLA Ops:
  7.2 0.7 all-gather.2.cloned.1.call-update
  7.9 0.7 broadcast_clamp_fusion
  8.9 0.7 broadcast_compare_fusion
  9.8 0.7 compare_select_fusion.2
  10.5 0.7 compare_and_fusion
  11.5 1.1 copy.62
  12.9 1.3 copy.64
  14.8 36.6 %all-gather.2.cloned.1.call-done = bf16[256,3,768]{2,0,1:T(8,128)(2,1)} async-done(((bf16[16,3,768]{2,0,1:T(8,128)(2,1)}), bf16[256,3,768]{2,0,1:T(8,128)(2,1)}) %all-gather.2.cloned.1.call-update) | async-done | bytes 1179664 | tf_op jit(solution)/shard_map/all_gather | solution.py:51
  51.4 2.3 copy.61
  53.7 0.7 gather_fusion
  54.6 1.2 gather_fusion.1
  55.9 0.5 reshape.256
  56.4 1.3 gather.18
  57.9 30.9 %reduce-window.6 = f32[6,20,3,6,128]{4,1,2,3,0:T(8,128)S(1)} reduce-window(f32[6,20,3,6,128]{4,1,2,3,0:T(8,128)S(1)} %copy.70, f32[]{:T(128)} %constant.84.clone.1), window={size=1x1x1x1x128 pad=0_0x0_0x0_0x0_0x127_0}, to_apply=%region_1.2 | reduce-window | flops 35112960 | bytes 2211844 | tf_op jit(solution)/shard_map/reduce-window
  89.3 1.0 copy.71
  90.4 0.5 broadcast_add_fusion
  91.1 0.6 reshape.257
  91.7 1.2 broadcast_select_fusion
  92.9 1.3 copy.63
  94.2 25.0 %fusion.19 = f32[1,360,469]{1,0,2:T(1,128)} fusion(bf16[1,360,768]{1,0,2:T(2,128)(2,1)S(1)} %copy.63, bf16[360,1,300]{0,1,2:T(2,128)(2,1)} %copy.64), kind=kOutput, calls=%fused_computation.50 | convolution fusion | flops 101304000 | bytes 1444320 | tf_op jit(solution)/shard_map/conv_general_dilated | solution.py:18
  119.1 2.3 copy.65
  121.8 2.3 fusion.6
  124.1 301.2 %gather_fusion.2 = f32[30720]{0:T(1024)S(1)} fusion(f32[6,20,469]{2,1,0:T(8,128)S(1)} %fusion.6, s32[30720]{0:T(1024)S(1)} %reshape.244), kind=kCustom, calls=%fused_computation.2 | custom fusion | bytes 614400 | tf_op jit(solution)/shard_map/jit(take_along_axis)/gather | solution.py:41
  425.7 32.2 %pmax.7 = f32[256]{0:T(256)} all-reduce(f32[256]{0:T(256)S(1)} %reduce_max.9), channel_id=1, replica_groups=mesh['groups'=2,'tmpl'=16] {'tmpl'}, use_global_device_ids=true, to_apply=%region_6.7 | all-reduce | flops 256 | bytes 2048 | tf_op jit(solution)/shard_map/pmax | solution.py:67
  (35 shorter events, 3.6 us)
Async XLA Ops:
  7.2 7.1 %copy-start = (bf16[6,20,3,300]{3,1,2,0:T(8,128)(2,1)S(1)}, bf16[6,20,3,300]{3,1,2,0:T(8,128)(2,1)}, u32[]{:S(2)}) copy-start(bf16[6,20,3,300]{3,1,2,0:T(8,128)(2,1)} %param.6) | copy-start | bytes 648004
  7.2 7.4 %copy-start.2 = (s32[6,20]{1,0:T(8,128)S(1)}, s32[6,20]{1,0:T(8,128)}, u32[]{:S(2)}) copy-start(s32[6,20]{1,0:T(8,128)} %param.9) | copy-start | bytes 1444
  7.2 44.2 %all-gather.2.cloned.1.call-start = ((), (), s32[]{:S(2)}) async-start(), calls=%async_computation | async-start | bytes 1253376 | tf_op jit(solution)/shard_map/all_gather | solution.py:51
  425.7 32.2 %copy-start.1 = (f32[6,256]{1,0:T(8,128)}, f32[6,256]{1,0:T(8,128)S(1)}, u32[]{:S(2)}) copy-start(f32[6,256]{1,0:T(8,128)S(1)} %fusion.10) | copy-start | bytes 18436
Sparse Core Ops, SparseCore 0:
  10.3 41.0 all-gather.1
where the time goes:
time: 465 us
  local copies, waits for them, and re-layouts  317 us (68%)
  other arithmetic  38.9 us (8%)
  waiting for transfers between devices  37.3 us (8%)
  blocking collectives  32.2 us (7%)
  matrix products  25 us (5%)
  between operations  14.3 us (3%)
    gather x2, local copies, waits for them, and re-layouts, batch_stack(): aligned = jnp.take_along_axis(channel_sum, offsets, axis=3)  301 us
    all_gather x1, waiting for transfers between devices, on_device(): block_rows = lax.all_gather(records, 'tmpl', axis=0, tiled=True)  36.6 us
    pmax x1, blocking collectives, on_device(): network_peak = lax.pmax(jnp.max(stack, axis=0), 'tmpl')  32.2 us
    another operation x3, other arithmetic  31.5 us
    conv_general_dilated x1, matrix products, batch_stack(): lax.conv_general_dilated(inputs_nch, filters, (1,), 'VALID', dimension_nu...  25 us
  transfers between devices with their start and end apart: 1, of which 1 were waited for; matrix products, arithmetic and copies ran while one was open for 1% of the time, Pallas kernels for 0%

commit v1 on v0

v1 whole, which is shorter than its diff:
```python
import functools

import jax
import jax.numpy as jnp
from jax import lax
from jax.experimental import pallas as pl
from jax.experimental.pallas import tpu as pltpu
from jax.sharding import PartitionSpec as P

OUT = 256
LANES = 128
VMEM = pltpu.VMEM
SMEM = pltpu.SMEM


def greet_all(n, me):
    barrier = pltpu.get_barrier_semaphore()

    def greet(d, carry):
        pl.semaphore_signal(
            barrier,
            inc=1,
            device_id={"tmpl": lax.rem(me + d, n)},
            device_id_type=pl.DeviceIdType.MESH,
        )
        return carry

    lax.fori_loop(1, n, greet, 0)
    pl.semaphore_wait(barrier, n - 1)


def push(src, dst, send, recv, peer):
    return pltpu.make_async_remote_copy(
        src_ref=src,
        dst_ref=dst,
        send_sem=send,
        recv_sem=recv,
        device_id={"tmpl": peer},
        device_id_type=pl.DeviceIdType.MESH,
    )


def fetch_kernel(n, stations, list_ref, rec_ref, out_ref, req_ref, asked, stage, s1, r1, s2, r2):
    me = lax.axis_index("tmpl")
    row = lax.broadcasted_iota(jnp.int32, (8, LANES), 0)
    comp = lax.rem(row, 4)

    def request(o, carry):
        wanted = jnp.where(row < 4, list_ref[0, o], list_ref[1, o])
        valid = jnp.logical_and(wanted >= 0, comp < 3)
        req_ref[o] = jnp.where(valid, comp * stations + wanted, -1)
        return carry

    lax.fori_loop(0, n, request, 0)
    greet_all(n, me)

    def ask(d):
        peer = lax.rem(me + d, n)
        return push(req_ref.at[peer], asked.at[me], s1.at[d], r1.at[d], peer)

    def give(d):
        peer = lax.rem(me + d, n)
        return push(stage.at[peer], out_ref.at[me], s2.at[d], r2.at[d], peer)

    def each(action):
        def body(d, carry):
            action(d)
            return carry

        lax.fori_loop(1, n, body, 0)

    each(lambda d: ask(d).start())
    asked[me] = req_ref[me]
    each(lambda d: ask(d).wait())
    rows = n * 8
    depth = rec_ref.shape[0]
    want = asked[...].reshape(rows, LANES)[:, :depth]
    lane = lax.broadcasted_iota(jnp.int32, (rows, depth), 1)
    onehot = jnp.where(want == lane, 1.0, 0.0).astype(jnp.bfloat16)
    picked = jnp.dot(onehot, rec_ref[...], preferred_element_type=jnp.float32)
    stage[...] = picked.reshape(n, 8, picked.shape[-1]).astype(jnp.bfloat16)
    each(lambda d: give(d).start())
    out_ref[me] = stage[me]
    each(lambda d: give(d).wait())


def fetch(wanted, rec_flat, stations):
    n = wanted.shape[1]
    width = rec_flat.shape[-1]
    return pl.pallas_call(
        functools.partial(fetch_kernel, n, stations),
        out_shape=jax.ShapeDtypeStruct((n, 8, width), jnp.bfloat16),
        in_specs=[pl.BlockSpec(memory_space=SMEM), pl.BlockSpec(memory_space=VMEM)],
        out_specs=pl.BlockSpec(memory_space=VMEM),
        scratch_shapes=[
            pltpu.VMEM((n, 8, LANES), jnp.int32),
            pltpu.VMEM((n, 8, LANES), jnp.int32),
            pltpu.VMEM((n, 8, width), jnp.bfloat16),
            pltpu.SemaphoreType.DMA((n,)),
            pltpu.SemaphoreType.DMA((n,)),
            pltpu.SemaphoreType.DMA((n,)),
            pltpu.SemaphoreType.DMA((n,)),
        ],
        compiler_params=pltpu.CompilerParams(collective_id=0, has_side_effects=True),
        name="fetch_rows",
    )(wanted, rec_flat)


def stack_kernel(
    taps, sets, nstat, slots_ref, moves_ref, rx_ref, tm_ref, stack_ref, peak_ref, comb, rolled, xt, hs, ht_ref
):
    n, _, width = rx_ref.shape
    pairs = sets * nstat
    row = lax.broadcasted_iota(jnp.int32, (8, width), 0)

    def ahead(v, k):
        return pltpu.roll(v, width - k, 1)

    def scale_owner(o, carry):
        x = rx_ref[o].astype(jnp.float32)
        run = x * x
        total = None
        done = 0
        size = 1
        pieces = []
        while size <= taps:
            if taps & size:
                pieces.append((size, run))
            size *= 2
            if size <= taps:
                run = run + ahead(run, size // 2)
        for size, piece in reversed(pieces):
            shifted = ahead(piece, done) if done else piece
            total = shifted if total is None else total + shifted
            done += size
        inv = lax.rsqrt(total / taps + 1e-05)
        first = jnp.where(row < 4, x, pltpu.roll(inv, 4, 0))
        second = jnp.where(row < 4, pltpu.roll(x, 4, 0), inv)
        comb[2 * o, :, :width] = first
        comb[2 * o + 1, :, :width] = second
        return carry

    lax.fori_loop(0, n, scale_owner, 0)

    used = xt.shape[1] // LANES
    lane = lax.broadcasted_iota(jnp.int32, (8, LANES), 1)

    def align_set(k, carry):
        for j in range(nstat):
            slot = slots_ref[k, j]
            move = moves_ref[k, j]
            base = move // LANES
            rest = move - base * LANES
            shift = (LANES - rest) & (LANES - 1)
            start = pl.multiple_of(base * LANES, LANES)
            keep = lane < LANES - rest
            tile = comb[slot, :, pl.ds(start, (used + 1) * LANES)]
            turned = [
                pltpu.roll(tile[:, v * LANES : (v + 1) * LANES], shift, 1) for v in range(used + 1)
            ]
            for v in range(used):
                rolled[k * nstat + j, :, v * LANES : (v + 1) * LANES] = jnp.where(
                    keep, turned[v], turned[v + 1]
                )
        return carry

    lax.fori_loop(0, sets, align_set, 0)

    for c in range(3):
        for v in range(used):
            block = rolled[:, c, v * LANES : (v + 1) * LANES]
            xt[c, v * LANES : (v + 1) * LANES, :] = block.T

    for c in range(3):
        for k in range(sets):
            hs[c, k * nstat : (k + 1) * nstat, :taps] = tm_ref[k, c].astype(jnp.float32)
        for v in range(ht_ref.shape[1] // LANES):
            ht_ref[c, v * LANES : (v + 1) * LANES, :] = hs[c, :, v * LANES : (v + 1) * LANES].T

    chans = []
    half = 128
    for t0 in range(0, OUT, half):
        chan = jnp.zeros((half, LANES), jnp.float32)
        for c in range(3):
            h = ht_ref[c, :taps, :]
            tscale = jnp.sqrt(jnp.sum(h * h, axis=0, keepdims=True) / taps + 1e-05)

            def tap_step(i, acc):
                for f in range(6):
                    tap = i * 6 + f
                    acc = acc + ht_ref[c, pl.ds(tap, 1), :] * xt[c, pl.ds(t0 + tap, half), :]
                return acc

            cc = lax.fori_loop(0, taps // 6, tap_step, jnp.zeros((half, LANES), jnp.float32))
            inv = rolled[:, 4 + c, t0 : t0 + half].T
            chan = chan + cc * (1.0 / (taps * tscale)) * inv
        chans.append(chan.T)
    whole = jnp.concatenate(chans, axis=1)
    rows = [
        jnp.sum(whole[k * nstat : (k + 1) * nstat], axis=0, keepdims=True) for k in range(sets)
    ]
    stack = jnp.concatenate(rows, axis=0)
    stack_ref[...] = stack
    peak_ref[...] = jnp.max(stack, axis=0, keepdims=True)


def local_stack(slots, moves, rx, kernels):
    taps = kernels.shape[-1]
    padded = -(-taps // LANES) * LANES
    n, _, width = rx.shape
    sets, nstat = slots.shape
    used = -(-(OUT + taps - 1) // LANES)
    return pl.pallas_call(
        functools.partial(stack_kernel, taps, sets, nstat),
        out_shape=(
            jax.ShapeDtypeStruct((sets, OUT), jnp.float32),
            jax.ShapeDtypeStruct((1, OUT), jnp.float32),
        ),
        in_specs=[
            pl.BlockSpec(memory_space=SMEM),
            pl.BlockSpec(memory_space=SMEM),
            pl.BlockSpec(memory_space=VMEM),
            pl.BlockSpec(memory_space=VMEM),
        ],
        out_specs=(pl.BlockSpec(memory_space=VMEM), pl.BlockSpec(memory_space=VMEM)),
        scratch_shapes=[
            pltpu.VMEM((2 * n, 8, width + LANES), jnp.float32),
            pltpu.VMEM((LANES, 8, used * LANES), jnp.float32),
            pltpu.VMEM((3, used * LANES, LANES), jnp.float32),
            pltpu.VMEM((3, LANES, padded), jnp.float32),
            pltpu.VMEM((3, padded, LANES), jnp.float32),
        ],
        compiler_params=pltpu.CompilerParams(vmem_limit_bytes=40 << 20),
        name="local_stack",
    )(slots, moves, rx, kernels)


def peak_kernel(n, peak_ref, out_ref, held, send, recv):
    me = lax.axis_index("tmpl")
    greet_all(n, me)

    def copy(d):
        peer = lax.rem(me + d, n)
        return push(peak_ref, held.at[me], send.at[d], recv.at[d], peer)

    def start(d, carry):
        copy(d).start()
        return carry

    def wait(d, carry):
        copy(d).wait()
        return carry

    lax.fori_loop(1, n, start, 0)
    held[me] = peak_ref[...]
    lax.fori_loop(1, n, wait, 0)
    out_ref[...] = jnp.max(held[...], axis=0)


def peak_all(peak, n):
    return pl.pallas_call(
        functools.partial(peak_kernel, n),
        out_shape=jax.ShapeDtypeStruct(peak.shape, jnp.float32),
        in_specs=[pl.BlockSpec(memory_space=VMEM)],
        out_specs=pl.BlockSpec(memory_space=VMEM),
        scratch_shapes=[
            pltpu.VMEM((n,) + peak.shape, jnp.float32),
            pltpu.SemaphoreType.DMA((n,)),
            pltpu.SemaphoreType.DMA((n,)),
        ],
        compiler_params=pltpu.CompilerParams(collective_id=1, has_side_effects=True),
        name="peak_all",
    )(peak)


def on_device(records, templates, fetch_list, cluster_slots, moveouts):
    n = fetch_list.shape[1]
    stations, comps, width = records.shape
    rec_flat = jnp.transpose(records, (1, 0, 2)).reshape(comps * stations, width)
    rx = fetch(jnp.transpose(fetch_list[0]), rec_flat, stations)
    kernels = jnp.transpose(templates, (0, 2, 1, 3))
    stack, peak = local_stack(cluster_slots, moveouts, rx, kernels)
    return stack, peak_all(peak, n).reshape(OUT)


def solution(mesh):
    placed = (
        P(("groups", "tmpl"), None, None),
        P("tmpl", None, None, None),
        P("tmpl", None, None),
        P("tmpl", None),
        P("tmpl", None),
    )
    return jax.shard_map(
        on_device,
        mesh=mesh,
        in_specs=placed,
        out_specs=(P(("groups", "tmpl"), None), P("groups")),
        check_vma=False,
    )
```

time: 465 us -> 53 us (0.11)
  local copies, waits for them, and re-layouts: 317 us -> 3.7 us
  Pallas kernels: 0 us -> 48.4 us
  other arithmetic: 38.9 us -> 0 us
  waiting for transfers between devices: 37.3 us -> 0 us
  blocking collectives: 32.2 us -> 0 us
  matrix products: 25 us -> 0 us
  between operations: 14.3 us -> 0.7 us
    gather x6 -> x0, local copies, waits for them, and re-layouts: 305 us -> none  [the longest x2 301 us: batch_stack(): aligned = jnp.take_along_axis(channel_sum, offsets, axis=3)]
    pallas_call x0 -> x3, Pallas kernels: none -> 48.4 us  [the longest x1 22.4 us: local_stack(): pl.pallas_call(functools.partial(stack_kernel, taps, sets, nstat), out_sh...]
    all_gather x1 -> x0, waiting for transfers between devices: 36.6 us -> none  [on_device(): block_rows = lax.all_gather(records, 'tmpl', axis=0, tiled=True)]
    pmax x1 -> x0, blocking collectives: 32.2 us -> none  [on_device(): network_peak = lax.pmax(jnp.max(stack, axis=0), 'tmpl')]
    another operation x3 -> x0, other arithmetic: 31.5 us -> none
    conv_general_dilated x1 -> x0, matrix products: 25 us -> none  [batch_stack(): lax.conv_general_dilated(inputs_nch, filters, (1,), 'VALID', dimension_nu...]
  transfers between devices with their start and end apart: 1 -> 0, of which waited for: 1 -> 0; matrix products, arithmetic and copies ran while one was open for 1% -> 0% of each run, Pallas kernels for 0% -> 0%
where the time goes in v1:
time: 53 us; the launch traced here: 52.8 us
  Pallas kernels  48.4 us (91%)
  local copies, waits for them, and re-layouts  3.7 us (7%)
  between operations  0.7 us (1%)
    pallas_call x1, Pallas kernels, local_stack(): pl.pallas_call(functools.partial(stack_kernel, taps, sets, nstat), out_sh...  22.4 us
    pallas_call x1, Pallas kernels, fetch(): pl.pallas_call(functools.partial(fetch_kernel, n, stations), out_shape=ja...  17.1 us
    pallas_call x1, Pallas kernels, peak_all(): pl.pallas_call(functools.partial(peak_kernel, n), out_shape=jax.ShapeDtyp...  8.86 us
    unnamed x13, local copies, waits for them, and re-layouts  3.7 us

profile of v1, /device:TPU:0, one launch (start us, length us, event | category | flops | bytes accessed | tf_op | source)
XLA Modules:
  0.0 52.8 jit_solution(17251951285448498218)
XLA Ops:
  0.6 0.0 copy-start.2
  0.6 0.0 copy-start.3
  0.7 17.1 %fetch_rows.1.rx_ref = bf16[16,8,768]{2,1,0:T(8,128)(2,1)} custom-call(s32[2,16]{1,0:T(2,128)} %bitcast.11, bf16[48,768]{1,0:T(8,128)(2,1)} %bitcast.9), custom_call_target="tpu_custom_call" | custom-call | tf_op jit(solution)/shard_map/fetch_rows/pallas_call | solution.py:90
  17.8 0.0 copy-done.2
  17.8 0.0 copy-done.3
  17.8 0.0 copy-start
  17.8 0.9 %copy-done = bf16[16,8,768]{2,1,0:T(8,128)(2,1)S(1)} copy-done((bf16[16,8,768]{2,1,0:T(8,128)(2,1)S(1)}, bf16[16,8,768]{2,1,0:T(8,128)(2,1)}, u32[]{:S(2)}) %copy-start) | copy-done | bytes 196632
  18.7 0.0 copy-start.1
  18.8 1.0 %copy-done.1 = bf16[6,20,3,300]{3,1,2,0:T(8,128)(2,1)S(1)} copy-done((bf16[6,20,3,300]{3,1,2,0:T(8,128)(2,1)S(1)}, bf16[6,20,3,300]{3,1,2,0:T(8,128)(2,1)}, u32[]{:S(2)}) %copy-start.1) | copy-done | bytes 216024
  19.7 22.4 %local_stack.1 = (f32[6,256]{1,0:T(8,128)}, f32[1,256]{1,0:T(1,128)S(1)}) custom-call(s32[6,20]{1,0:T(8,128)S(1)} %copy-done.2, s32[6,20]{1,0:T(8,128)S(1)} %copy-done.3, bf16[16,8,768]{2,1,0:T(8,128)(2,1)S(1)} %copy-done, bf16[6,3,20,300]{3,2,1,0:T(8,128)(2,1)S(1)} %bitcast.8), custom_call_target="tpu_custom_call" | custom-call | tf_op jit(solution)/shard_map/local_stack/pallas_call | solution.py:213
  42.1 0.0 copy-start.4
  42.1 0.6 %copy-done.4 = f32[1,256]{1,0:T(1,128)} copy-done((f32[1,256]{1,0:T(1,128)}, f32[1,256]{1,0:T(1,128)S(1)}, u32[]{:S(2)}) %copy-start.4) | copy-done | bytes 1048
  42.6 8.9 %peak_all.1 = f32[1,256]{1,0:T(1,128)} custom-call(f32[1,256]{1,0:T(1,128)} %copy-done.4), custom_call_target="tpu_custom_call" | custom-call | tf_op jit(solution)/shard_map/peak_all/pallas_call | solution.py:261
  51.5 0.0 copy-start.5
  51.5 0.7 %copy-done.5 = f32[1,256]{1,0:T(1,128)S(1)} copy-done((f32[1,256]{1,0:T(1,128)S(1)}, f32[1,256]{1,0:T(1,128)}, u32[]{:S(2)}) %copy-start.5) | copy-done | bytes 1048
  52.2 0.6 %copy.8 = f32[256]{0:T(256)} copy(f32[256]{0:T(256)S(1)} %bitcast.10) | data formatting | bytes 2048
Async XLA Ops:
  0.6 17.2 %copy-start.2 = (s32[6,20]{1,0:T(8,128)S(1)}, s32[6,20]{1,0:T(8,128)}, u32[]{:S(2)}) copy-start(s32[6,20]{1,0:T(8,128)} %slots_ref.1) | copy-start | bytes 1444
  0.6 17.2 %copy-start.3 = (s32[6,20]{1,0:T(8,128)S(1)}, s32[6,20]{1,0:T(8,128)}, u32[]{:S(2)}) copy-start(s32[6,20]{1,0:T(8,128)} %moves_ref.1) | copy-start | bytes 1444
  17.8 0.9 %copy-start = (bf16[16,8,768]{2,1,0:T(8,128)(2,1)S(1)}, bf16[16,8,768]{2,1,0:T(8,128)(2,1)}, u32[]{:S(2)}) copy-start(bf16[16,8,768]{2,1,0:T(8,128)(2,1)} %fetch_rows.1.rx_ref) | copy-start | bytes 589828
  18.7 1.0 %copy-start.1 = (bf16[6,20,3,300]{3,1,2,0:T(8,128)(2,1)S(1)}, bf16[6,20,3,300]{3,1,2,0:T(8,128)(2,1)}, u32[]{:S(2)}) copy-start(bf16[6,20,3,300]{3,1,2,0:T(8,128)(2,1)} %param.6) | copy-start | bytes 648004
  42.1 0.6 %copy-start.4 = (f32[1,256]{1,0:T(1,128)}, f32[1,256]{1,0:T(1,128)S(1)}, u32[]{:S(2)}) copy-start(f32[1,256]{1,0:T(1,128)S(1)} %get-tuple-element.5.peak_ref) | copy-start | bytes 3076
  51.5 0.7 %copy-start.5 = (f32[1,256]{1,0:T(1,128)S(1)}, f32[1,256]{1,0:T(1,128)}, u32[]{:S(2)}) copy-start(f32[1,256]{1,0:T(1,128)} %peak_all.1) | copy-start | bytes 3076

commit v2 on v0

v2 whole, which is shorter than its diff:
```python
import functools

import jax
import jax.numpy as jnp
from jax import lax
from jax.experimental import pallas as pl
from jax.experimental.pallas import tpu as pltpu
from jax.sharding import PartitionSpec as P

OUT = 256
LANES = 128


def push(src, dst, send, recv, peer):
    return pltpu.make_async_remote_copy(
        src_ref=src,
        dst_ref=dst,
        send_sem=send,
        recv_sem=recv,
        device_id={"tmpl": peer},
        device_id_type=pl.DeviceIdType.MESH,
    )


def each(low, high, action):
    def body(d, carry):
        action(d)
        return carry

    lax.fori_loop(low, high, body, 0)


def kernel(
    n, stations, sets, nstat, taps,
    list_ref, slots_ref, moves_ref, rec_hbm, tm_hbm,
    stack_ref, peak_ref,
    rec_ref, tm_ref, req_ref, asked, stage, rx_ref, ids, xs, ys, es, xt, it, hs, ht, tinv, chan, mine, held,
    local, s1, r1, s2, r2, s3, r3,
):
    me = lax.axis_index("tmpl")
    tm_copy = pltpu.make_async_copy(tm_hbm, tm_ref, local.at[0])
    rec_copy = pltpu.make_async_copy(rec_hbm, rec_ref, local.at[1])
    tm_copy.start()
    rec_copy.start()

    barrier = pltpu.get_barrier_semaphore()
    each(1, n, lambda d: pl.semaphore_signal(
        barrier, inc=1, device_id={"tmpl": lax.rem(me + d, n)},
        device_id_type=pl.DeviceIdType.MESH))

    row = lax.broadcasted_iota(jnp.int32, (8, LANES), 0)
    comp = lax.rem(row, 4)

    def request(o):
        wanted = jnp.where(row < 4, list_ref[0, o], list_ref[1, o])
        valid = jnp.logical_and(wanted >= 0, comp < 3)
        req_ref[o] = jnp.where(valid, comp * stations + wanted, -1)

    each(0, n, request)
    pl.semaphore_wait(barrier, n - 1)

    def ask(d):
        peer = lax.rem(me + d, n)
        return push(req_ref.at[peer], asked.at[me], s1.at[d], r1.at[d], peer)

    def give(d):
        peer = lax.rem(me + d, n)
        return push(stage.at[peer], rx_ref.at[me], s2.at[d], r2.at[d], peer)

    def tell(d):
        peer = lax.rem(me + d, n)
        return push(mine, held.at[me], s3.at[d], r3.at[d], peer)

    each(1, n, lambda d: ask(d).start())
    ids[0:8, :] = jnp.full((8, LANES), -1, jnp.int32)
    ids[8:16, :] = jnp.zeros((8, LANES), jnp.int32)
    for k in range(sets):
        ids[0:1, k * nstat : (k + 1) * nstat] = slots_ref[k : k + 1, :]
        ids[8:9, k * nstat : (k + 1) * nstat] = moves_ref[k : k + 1, :]
    asked[me] = req_ref[me]

    tm_copy.wait()
    for c in range(3):
        for k in range(sets):
            hs[c, k * nstat : (k + 1) * nstat, :taps] = tm_ref[k, c].astype(jnp.float32)
        for v in range(ht.shape[1] // LANES):
            ht[c, v * LANES : (v + 1) * LANES, :] = hs[c, :, v * LANES : (v + 1) * LANES].T
        h = ht[c, :taps, :]
        tscale = jnp.sqrt(jnp.sum(h * h, axis=0, keepdims=True) / taps + 1e-05)
        tinv[c] = jnp.broadcast_to(1.0 / (taps * tscale), (8, LANES))

    rec_copy.wait()
    each(1, n, lambda d: ask(d).wait())
    rows = n * 8
    depth, width = rec_ref.shape
    want = asked[...].reshape(rows, LANES)[:, :depth]
    spot = lax.broadcasted_iota(jnp.int32, (rows, depth), 1)
    onehot = jnp.where(want == spot, 1.0, 0.0).astype(jnp.bfloat16)
    picked = jnp.dot(onehot, rec_ref[...], preferred_element_type=jnp.float32)
    stage[...] = picked.reshape(n, 8, width).astype(jnp.bfloat16)
    each(1, n, lambda d: give(d).start())
    rx_ref[me] = stage[me]

    each(1, n, lambda d: give(d).wait())

    spot = lax.broadcasted_iota(jnp.int32, (rows, LANES), 0)
    slot = ids[0:1, :] * 4
    chosen = jnp.concatenate(
        [jnp.where(spot == slot + c, 1.0, 0.0) for c in range(3)], axis=1
    ).astype(jnp.bfloat16)
    got = rx_ref[...].reshape(rows, width)
    picked = lax.dot_general(
        got, chosen, (((0,), (0,)), ((), ())), preferred_element_type=jnp.float32
    )
    for c in range(3):
        xs[c, :width, :] = picked[:, c * LANES : (c + 1) * LANES]

    moves = jnp.broadcast_to(ids[8:9, :], (8, LANES))
    bits = {b: (moves & b) != 0 for b in (128, 64, 32, 16, 8, 4, 2, 1)}

    def choose(bit, one, zero):
        return [jnp.where(bits[bit], p, q) for p, q in zip(one, zero)]

    def coarse(c, b):
        at = b * 64
        tiles = [xs[c, pl.ds(at + 8 * q, 8), :] for q in range(39)]
        for bit in (128, 64, 32, 16, 8):
            tiles = choose(bit, tiles[bit // 8 :], tiles[: -(bit // 8)])
        for q, tile in enumerate(tiles):
            ys[pl.ds(at + 8 * q, 8), :] = tile

    def fine(c, b):
        for q in range(5):
            at = b * 40 + 8 * q
            tiles = [ys[pl.ds(at + i, 8), :] for i in range(8)]
            for bit in (4, 2, 1):
                tiles = choose(bit, tiles[bit : 2 * bit], tiles[:bit])
            xt[c, pl.ds(at, 8), :] = tiles[0]

    def squares(c, at, count):
        total = None
        for i in range(count):
            x = xt[c, pl.ds(at + i, 8), :]
            total = x * x if total is None else total + x * x
        return total

    def eights(c, b):
        for q in range(4):
            at = b * 32 + 8 * q
            es[pl.ds(at, 8), :] = squares(c, at, 8)

    steps = taps // 8
    rest = taps - steps * 8

    def scales(c):
        run = [es[8 * q : 8 * q + 8, :] for q in range(OUT // 8 + steps - 1)]
        pieces = []
        size = 1
        while size <= steps:
            if steps & size:
                pieces.append((size, run))
            run = [p + q for p, q in zip(run, run[size:])]
            size *= 2
        for q in range(OUT // 8):
            done = 0
            total = squares(c, 8 * (q + steps), rest) if rest else None
            for size, piece in reversed(pieces):
                term = piece[q + done]
                total = term if total is None else total + term
                done += size
            it[c, 8 * q : 8 * q + 8, :] = lax.rsqrt(total / taps + 1e-05) * tinv[c]

    chan[...] = jnp.zeros_like(chan)
    tiles = 16
    span = tiles * 8

    def component(c):
        each(0, 9, lambda b: coarse(c, b))
        each(0, 14, lambda b: fine(c, b))
        each(0, 17, lambda b: eights(c, b))
        scales(c)
        for t0 in range(0, OUT, span):

            def phase(f, acc):
                win = [xt[c, pl.ds(t0 + f + 8 * q, 8), :] for q in range(tiles)]
                for e in range(steps):
                    h = jnp.broadcast_to(ht[c, pl.ds(f + 8 * e, 1), :], (8, LANES))
                    acc = tuple(a + h * w for a, w in zip(acc, win))
                    if e < steps - 1:
                        win = win[1:] + [xt[c, pl.ds(t0 + f + 8 * (tiles + e), 8), :]]
                return acc

            acc = tuple(jnp.zeros((8, LANES), jnp.float32) for _ in range(tiles))
            acc = lax.fori_loop(0, 8, phase, acc)
            for tap in range(taps // 8 * 8, taps):
                h = jnp.broadcast_to(ht[c, pl.ds(tap, 1), :], (8, LANES))
                acc = tuple(
                    a + h * xt[c, pl.ds(t0 + tap + 8 * q, 8), :] for q, a in enumerate(acc)
                )
            for q in range(tiles):
                at = pl.ds(t0 + 8 * q, 8)
                chan[at, :] += acc[q] * it[c, at, :]

    each(0, 3, component)
    flat = jnp.concatenate([chan[v : v + LANES].T for v in range(0, OUT, LANES)], axis=1)
    stack = jnp.concatenate(
        [jnp.sum(flat[k * nstat : (k + 1) * nstat], axis=0, keepdims=True) for k in range(sets)],
        axis=0,
    )
    stack_ref[...] = stack
    best = jnp.max(stack, axis=0, keepdims=True)
    mine[...] = best
    each(1, n, lambda d: tell(d).start())
    held[me] = best
    each(1, n, lambda d: tell(d).wait())
    peak_ref[...] = jnp.max(held[...], axis=0)


def on_device(records, templates, fetch_list, cluster_slots, moveouts):
    n = fetch_list.shape[1]
    stations, comps, width = records.shape
    sets, nstat = cluster_slots.shape
    taps = templates.shape[-1]
    padded = -(-taps // LANES) * LANES
    used = -(-(OUT + taps - 1) // LANES)
    rec_flat = jnp.transpose(records, (1, 0, 2)).reshape(comps * stations, width)
    kernels = jnp.transpose(templates, (0, 2, 1, 3))
    vmem = pl.BlockSpec(memory_space=pltpu.VMEM)
    smem = pl.BlockSpec(memory_space=pltpu.SMEM)
    far = pl.BlockSpec(memory_space=pltpu.HBM)
    sems = pltpu.SemaphoreType.DMA((n,))
    stack, peak = pl.pallas_call(
        functools.partial(kernel, n, stations, sets, nstat, taps),
        out_shape=(
            jax.ShapeDtypeStruct((sets, OUT), jnp.float32),
            jax.ShapeDtypeStruct((1, OUT), jnp.float32),
        ),
        in_specs=[smem, vmem, vmem, far, far],
        out_specs=(vmem, vmem),
        scratch_shapes=[
            pltpu.VMEM(rec_flat.shape, jnp.bfloat16),
            pltpu.VMEM(kernels.shape, jnp.bfloat16),
            pltpu.VMEM((n, 8, LANES), jnp.int32),
            pltpu.VMEM((n, 8, LANES), jnp.int32),
            pltpu.VMEM((n, 8, width), jnp.bfloat16),
            pltpu.VMEM((n, 8, width), jnp.bfloat16),
            pltpu.VMEM((16, LANES), jnp.int32),
            pltpu.VMEM((3, 832, LANES), jnp.float32),
            pltpu.VMEM((576, LANES), jnp.float32),
            pltpu.VMEM((544, LANES), jnp.float32),
            pltpu.VMEM((3, used * LANES, LANES), jnp.float32),
            pltpu.VMEM((3, OUT, LANES), jnp.float32),
            pltpu.VMEM((3, LANES, padded), jnp.float32),
            pltpu.VMEM((3, padded, LANES), jnp.float32),
            pltpu.VMEM((3, 8, LANES), jnp.float32),
            pltpu.VMEM((OUT, LANES), jnp.float32),
            pltpu.VMEM((1, OUT), jnp.float32),
            pltpu.VMEM((n, 1, OUT), jnp.float32),
            pltpu.SemaphoreType.DMA((2,)),
            sems, sems, sems, sems, sems, sems,
        ],
        compiler_params=pltpu.CompilerParams(
            collective_id=0, has_side_effects=True, vmem_limit_bytes=40 << 20
        ),
        name="network_stack",
    )(jnp.transpose(fetch_list[0]), cluster_slots, moveouts, rec_flat, kernels)
    return stack, peak.reshape(OUT)


def solution(mesh):
    placed = (
        P(("groups", "tmpl"), None, None),
        P("tmpl", None, None, None),
        P("tmpl", None, None),
        P("tmpl", None),
        P("tmpl", None),
    )
    return jax.shard_map(
        on_device,
        mesh=mesh,
        in_specs=placed,
        out_specs=(P(("groups", "tmpl"), None), P("groups")),
        check_vma=False,
    )
```

time: 465 us -> 37.5 us (0.08)
  local copies, waits for them, and re-layouts: 317 us -> 4.39 us
  other arithmetic: 38.9 us -> 0 us
  waiting for transfers between devices: 37.3 us -> 0 us
  blocking collectives: 32.2 us -> 0 us
  Pallas kernels: 0 us -> 32.1 us
  matrix products: 25 us -> 0 us
  between operations: 14.3 us -> 0.66 us
    gather x6 -> x0, local copies, waits for them, and re-layouts: 305 us -> none  [the longest x2 301 us: batch_stack(): aligned = jnp.take_along_axis(channel_sum, offsets, axis=3)]
    all_gather x1 -> x0, waiting for transfers between devices: 36.6 us -> none  [on_device(): block_rows = lax.all_gather(records, 'tmpl', axis=0, tiled=True)]
    pmax x1 -> x0, blocking collectives: 32.2 us -> none  [on_device(): network_peak = lax.pmax(jnp.max(stack, axis=0), 'tmpl')]
    pallas_call x0 -> x1, Pallas kernels: none -> 32.1 us  [on_device(): pl.pallas_call(functools.partial(kernel, n, stations, sets, nstat, taps),...]
    another operation x3 -> x0, other arithmetic: 31.5 us -> none
    conv_general_dilated x1 -> x0, matrix products: 25 us -> none  [batch_stack(): lax.conv_general_dilated(inputs_nch, filters, (1,), 'VALID', dimension_nu...]
  transfers between devices with their start and end apart: 1 -> 0, of which waited for: 1 -> 0; matrix products, arithmetic and copies ran while one was open for 1% -> 0% of each run, Pallas kernels for 0% -> 0%
where the time goes in v2:
time: 37.5 us; the launch traced here: 37.2 us
  Pallas kernels  32.1 us (86%)
  local copies, waits for them, and re-layouts  4.39 us (12%)
  between operations  0.66 us (2%)
    pallas_call x1, Pallas kernels, on_device(): pl.pallas_call(functools.partial(kernel, n, stations, sets, nstat, taps),...  32.1 us
    unnamed x12, local copies, waits for them, and re-layouts  4.39 us

profile of v2, /device:TPU:0, one launch (start us, length us, event | category | flops | bytes accessed | tf_op | source)
XLA Modules:
  0.0 37.2 jit_solution(7599746051829842384)
XLA Ops:
  0.6 0.0 copy-start.2
  0.6 0.0 copy-start.4
  0.7 0.7 %copy-done.2 = s32[6,20]{1,0:T(8,128)S(1)} copy-done((s32[6,20]{1,0:T(8,128)S(1)}, s32[6,20]{1,0:T(8,128)}, u32[]{:S(2)}) %copy-start.2) | copy-done | bytes 504
  1.3 0.0 copy-done.4
  1.3 0.0 copy-start
  1.3 1.0 %copy-done = bf16[6,20,3,300]{3,1,2,0:T(8,128)(2,1)S(1)} copy-done((bf16[6,20,3,300]{3,1,2,0:T(8,128)(2,1)S(1)}, bf16[6,20,3,300]{3,1,2,0:T(8,128)(2,1)}, u32[]{:S(2)}) %copy-start) | copy-done | bytes 216024
  2.3 0.0 copy-start.1
  2.3 0.9 %copy-done.1 = bf16[16,3,768]{2,0,1:T(8,128)(2,1)S(1)} copy-done((bf16[16,3,768]{2,0,1:T(8,128)(2,1)S(1)}, bf16[16,3,768]{2,0,1:T(8,128)(2,1)}, u32[]{:S(2)}) %copy-start.1) | copy-done | bytes 73752
  3.2 0.0 copy-start.3
  3.2 0.7 %copy-done.3 = s32[6,20]{1,0:T(8,128)S(1)} copy-done((s32[6,20]{1,0:T(8,128)S(1)}, s32[6,20]{1,0:T(8,128)}, u32[]{:S(2)}) %copy-start.3) | copy-done | bytes 504
  3.9 32.1 %network_stack.1 = (f32[6,256]{1,0:T(8,128)S(1)}, f32[1,256]{1,0:T(1,128)S(1)}) custom-call(s32[2,16]{1,0:T(2,128)S(1)} %bitcast.10, s32[6,20]{1,0:T(8,128)S(1)} %copy-done.2, s32[6,20]{1,0:T(8,128)S(1)} %copy-done.3, bf16[48,768]{1,0:T(8,128)(2,1)S(1)} %bitcast.9, bf16[6,3,20,300]{3,2,1,0:T(8,128)(2,1)S(1)} %bitcast.8), custom_call_target="tpu_custom_call" | custom-call | tf_op jit(solution)/shard_map/network_stack/pallas_call | solution.py:232
  36.0 0.6 %copy.9 = f32[6,256]{1,0:T(8,128)} copy(f32[6,256]{1,0:T(8,128)S(1)} %get-tuple-element.8) | data formatting | bytes 12288
  36.6 0.6 %copy.10 = f32[256]{0:T(256)} copy(f32[256]{0:T(256)S(1)} %bitcast.11) | data formatting | bytes 2048
Async XLA Ops:
  0.6 0.7 %copy-start.2 = (s32[6,20]{1,0:T(8,128)S(1)}, s32[6,20]{1,0:T(8,128)}, u32[]{:S(2)}) copy-start(s32[6,20]{1,0:T(8,128)} %slots_ref.1) | copy-start | bytes 1444
  0.6 0.7 %copy-start.4 = (s32[1,16,2]{1,2,0:T(2,128)S(1)}, s32[1,16,2]{1,2,0:T(2,128)}, u32[]{:S(2)}) copy-start(s32[1,16,2]{1,2,0:T(2,128)} %param.7) | copy-start | bytes 388
  1.3 1.0 %copy-start = (bf16[6,20,3,300]{3,1,2,0:T(8,128)(2,1)S(1)}, bf16[6,20,3,300]{3,1,2,0:T(8,128)(2,1)}, u32[]{:S(2)}) copy-start(bf16[6,20,3,300]{3,1,2,0:T(8,128)(2,1)} %param.6) | copy-start | bytes 648004
  2.3 0.9 %copy-start.1 = (bf16[16,3,768]{2,0,1:T(8,128)(2,1)S(1)}, bf16[16,3,768]{2,0,1:T(8,128)(2,1)}, u32[]{:S(2)}) copy-start(bf16[16,3,768]{2,0,1:T(8,128)(2,1)} %param.5) | copy-start | bytes 221188
  3.2 0.7 %copy-start.3 = (s32[6,20]{1,0:T(8,128)S(1)}, s32[6,20]{1,0:T(8,128)}, u32[]{:S(2)}) copy-start(s32[6,20]{1,0:T(8,128)} %moves_ref.1) | copy-start | bytes 1444

commit v3 on v2

--- a/solution.py
+++ b/solution.py
@@ -32,16 +32,22 @@
 
 def kernel(
     n, stations, sets, nstat, taps,
-    list_ref, slots_ref, moves_ref, rec_hbm, tm_hbm,
+    list_hbm, slots_hbm, moves_hbm, rec_hbm, tm_hbm,
     stack_ref, peak_ref,
-    rec_ref, tm_ref, req_ref, asked, stage, rx_ref, ids, xs, ys, es, xt, it, hs, ht, tinv, chan, mine, held,
+    list_ref, slots_ref, moves_ref, rec_ref, tm_ref, req_ref, asked, stage, rx_ref, ids, xs, ys, es, xt, it, hs, ht, tinv, chan, mine, held,
     local, s1, r1, s2, r2, s3, r3,
 ):
     me = lax.axis_index("tmpl")
     tm_copy = pltpu.make_async_copy(tm_hbm, tm_ref, local.at[0])
     rec_copy = pltpu.make_async_copy(rec_hbm, rec_ref, local.at[1])
+    list_copy = pltpu.make_async_copy(list_hbm, list_ref, local.at[2])
+    slots_copy = pltpu.make_async_copy(slots_hbm, slots_ref, local.at[3])
+    moves_copy = pltpu.make_async_copy(moves_hbm, moves_ref, local.at[4])
+    list_copy.start()
+    rec_copy.start()
+    slots_copy.start()
+    moves_copy.start()
     tm_copy.start()
-    rec_copy.start()
 
     barrier = pltpu.get_barrier_semaphore()
     each(1, n, lambda d: pl.semaphore_signal(
@@ -56,6 +62,7 @@
         valid = jnp.logical_and(wanted >= 0, comp < 3)
         req_ref[o] = jnp.where(valid, comp * stations + wanted, -1)
 
+    list_copy.wait()
     each(0, n, request)
     pl.semaphore_wait(barrier, n - 1)
 
@@ -74,6 +81,8 @@
     each(1, n, lambda d: ask(d).start())
     ids[0:8, :] = jnp.full((8, LANES), -1, jnp.int32)
     ids[8:16, :] = jnp.zeros((8, LANES), jnp.int32)
+    slots_copy.wait()
+    moves_copy.wait()
     for k in range(sets):
         ids[0:1, k * nstat : (k + 1) * nstat] = slots_ref[k : k + 1, :]
         ids[8:9, k * nstat : (k + 1) * nstat] = moves_ref[k : k + 1, :]
@@ -226,7 +235,6 @@
     rec_flat = jnp.transpose(records, (1, 0, 2)).reshape(comps * stations, width)
     kernels = jnp.transpose(templates, (0, 2, 1, 3))
     vmem = pl.BlockSpec(memory_space=pltpu.VMEM)
-    smem = pl.BlockSpec(memory_space=pltpu.SMEM)
     far = pl.BlockSpec(memory_space=pltpu.HBM)
     sems = pltpu.SemaphoreType.DMA((n,))
     stack, peak = pl.pallas_call(
@@ -235,9 +243,12 @@
             jax.ShapeDtypeStruct((sets, OUT), jnp.float32),
             jax.ShapeDtypeStruct((1, OUT), jnp.float32),
         ),
-        in_specs=[smem, vmem, vmem, far, far],
+        in_specs=[far] * 5,
         out_specs=(vmem, vmem),
         scratch_shapes=[
+            pltpu.SMEM((fetch_list.shape[2], n), jnp.int32),
+            pltpu.VMEM(cluster_slots.shape, jnp.int32),
+            pltpu.VMEM(moveouts.shape, jnp.int32),
             pltpu.VMEM(rec_flat.shape, jnp.bfloat16),
             pltpu.VMEM(kernels.shape, jnp.bfloat16),
             pltpu.VMEM((n, 8, LANES), jnp.int32),
@@ -256,11 +267,11 @@
             pltpu.VMEM((OUT, LANES), jnp.float32),
             pltpu.VMEM((1, OUT), jnp.float32),
             pltpu.VMEM((n, 1, OUT), jnp.float32),
-            pltpu.SemaphoreType.DMA((2,)),
+            pltpu.SemaphoreType.DMA((5,)),
             sems, sems, sems, sems, sems, sems,
         ],
         compiler_params=pltpu.CompilerParams(
-            collective_id=0, has_side_effects=True, vmem_limit_bytes=40 << 20
+            collective_id=0, has_side_effects=True, vmem_limit_bytes=60 << 20
         ),
         name="network_stack",
     )(jnp.transpose(fetch_list[0]), cluster_slots, moveouts, rec_flat, kernels)

time: 37.5 us -> 34.7 us (0.925)
  local copies, waits for them, and re-layouts: 4.39 us -> 1.86 us
    unnamed x12 -> x4, local copies, waits for them, and re-layouts: 4.39 us -> 1.86 us
where the time goes in v3:
time: 34.7 us; the launch traced here: 34.6 us
  Pallas kernels  32 us (92%)
  local copies, waits for them, and re-layouts  1.86 us (5%)
  between operations  0.65 us (2%)
    pallas_call x1, Pallas kernels, on_device(): pl.pallas_call(functools.partial(kernel, n, stations, sets, nstat, taps),...  32 us
    unnamed x4, local copies, waits for them, and re-layouts  1.86 us

profile of v3, /device:TPU:0, one launch (start us, length us, event | category | flops | bytes accessed | tf_op | source)
XLA Modules:
  0.0 34.6 jit_solution(11126708866708517414)
XLA Ops:
  0.6 32.0 %network_stack.1 = (f32[6,256]{1,0:T(8,128)}, f32[1,256]{1,0:T(1,128)}) custom-call(s32[2,16]{1,0:T(2,128)} %bitcast.10, s32[6,20]{1,0:T(8,128)} %slots_hbm.1, s32[6,20]{1,0:T(8,128)} %moves_hbm.1, bf16[48,768]{1,0:T(8,128)(2,1)} %bitcast.9, bf16[6,3,20,300]{3,2,1,0:T(8,128)(2,1)} %bitcast.8), custom_call_target="tpu_custom_call" | custom-call | tf_op jit(solution)/shard_map/network_stack/pallas_call | solution.py:240
  32.7 0.0 copy-start
  32.7 1.3 %copy.9 = f32[6,256]{1,0:T(8,128)} copy(f32[6,256]{1,0:T(8,128)} %get-tuple-element.8) | data formatting | bytes 12288
  34.0 0.0 copy-done
  34.0 0.6 %copy.10 = f32[256]{0:T(256)} copy(f32[256]{0:T(256)S(1)} %bitcast.11) | data formatting | bytes 2048
Async XLA Ops:
  32.7 1.3 %copy-start = (f32[1,256]{1,0:T(1,128)S(1)}, f32[1,256]{1,0:T(1,128)}, u32[]{:S(2)}) copy-start(f32[1,256]{1,0:T(1,128)} %get-tuple-element.5) | copy-start | bytes 3076

commit v4 on v3

--- a/solution.py
+++ b/solution.py
@@ -34,7 +34,7 @@
     n, stations, sets, nstat, taps,
     list_hbm, slots_hbm, moves_hbm, rec_hbm, tm_hbm,
     stack_ref, peak_ref,
-    list_ref, slots_ref, moves_ref, rec_ref, tm_ref, req_ref, asked, stage, rx_ref, ids, xs, ys, es, xt, it, hs, ht, tinv, chan, mine, held,
+    list_ref, slots_ref, moves_ref, rec_ref, tm_ref, req_ref, asked, stage, rx_ref, ids, xs, ys, es, xt, it, hs, ht, tinv, xa, ha, af, line, chan, mine, held,
     local, s1, r1, s2, r2, s3, r3,
 ):
     me = lax.axis_index("tmpl")
@@ -49,17 +49,18 @@
     moves_copy.start()
     tm_copy.start()
 
+    rx_ref[...] = jnp.zeros_like(rx_ref)
     barrier = pltpu.get_barrier_semaphore()
     each(1, n, lambda d: pl.semaphore_signal(
         barrier, inc=1, device_id={"tmpl": lax.rem(me + d, n)},
         device_id_type=pl.DeviceIdType.MESH))
 
     row = lax.broadcasted_iota(jnp.int32, (8, LANES), 0)
-    comp = lax.rem(row, 4)
+    comp = jnp.where(row < 3, row, row - 3)
 
     def request(o):
-        wanted = jnp.where(row < 4, list_ref[0, o], list_ref[1, o])
-        valid = jnp.logical_and(wanted >= 0, comp < 3)
+        wanted = jnp.where(row < 3, list_ref[0, o], list_ref[1, o])
+        valid = jnp.logical_and(wanted >= 0, row < 6)
         req_ref[o] = jnp.where(valid, comp * stations + wanted, -1)
 
     list_copy.wait()
@@ -72,7 +73,7 @@
 
     def give(d):
         peer = lax.rem(me + d, n)
-        return push(stage.at[peer], rx_ref.at[me], s2.at[d], r2.at[d], peer)
+        return push(stage.at[peer, pl.ds(0, 6)], rx_ref.at[me, pl.ds(0, 6)], s2.at[d], r2.at[d], peer)
 
     def tell(d):
         peer = lax.rem(me + d, n)
@@ -94,6 +95,11 @@
             hs[c, k * nstat : (k + 1) * nstat, :taps] = tm_ref[k, c].astype(jnp.float32)
         for v in range(ht.shape[1] // LANES):
             ht[c, v * LANES : (v + 1) * LANES, :] = hs[c, :, v * LANES : (v + 1) * LANES].T
+        h0 = ht[c, pl.ds(0, taps // 2, stride=2), :]
+        h1 = ht[c, pl.ds(1, taps // 2, stride=2), :]
+        ha[c, 0, : taps // 2, :] = h0 + h1
+        ha[c, 1, : taps // 2, :] = h0
+        ha[c, 2, : taps // 2, :] = h1
         h = ht[c, :taps, :]
         tscale = jnp.sqrt(jnp.sum(h * h, axis=0, keepdims=True) / taps + 1e-05)
         tinv[c] = jnp.broadcast_to(1.0 / (taps * tscale), (8, LANES))
@@ -113,7 +119,7 @@
     each(1, n, lambda d: give(d).wait())
 
     spot = lax.broadcasted_iota(jnp.int32, (rows, LANES), 0)
-    slot = ids[0:1, :] * 4
+    slot = (ids[0:1, :] >> 1) * 8 + (ids[0:1, :] & 1) * 3
     chosen = jnp.concatenate(
         [jnp.where(spot == slot + c, 1.0, 0.0) for c in range(3)], axis=1
     ).astype(jnp.bfloat16)
@@ -181,37 +187,57 @@
 
     chan[...] = jnp.zeros_like(chan)
     tiles = 16
-    span = tiles * 8
+
+    def parts(c, b):
+        for q in range(5):
+            at = b * 40 + 8 * q
+            x0 = xt[c, pl.ds(2 * at, 8, stride=2), :]
+            x1 = xt[c, pl.ds(2 * at + 1, 8, stride=2), :]
+            x2 = xt[c, pl.ds(2 * at + 2, 8, stride=2), :]
+            xa[0, pl.ds(at, 8), :] = x1
+            xa[1, pl.ds(at, 8), :] = x0 - x1
+            xa[2, pl.ds(at, 8), :] = x2 - x1
+
+    def correlate(c, m):
+        def phase(count):
+            def body(f, acc):
+                win = [xa[m, pl.ds(f + 8 * q, 8), :] for q in range(tiles)]
+                for e in range(count):
+                    h = jnp.broadcast_to(ha[c, m, pl.ds(f + 8 * e, 1), :], (8, LANES))
+                    acc = tuple(a + h * w for a, w in zip(acc, win))
+                    if e < count - 1:
+                        win = win[1:] + [xa[m, pl.ds(f + 8 * (tiles + e), 8), :]]
+                return acc
+
+            return body
+
+        taken = taps // 2
+        acc = tuple(jnp.zeros((8, LANES), jnp.float32) for _ in range(tiles))
+        acc = lax.fori_loop(0, taken % 8, phase(taken // 8 + 1), acc)
+        acc = lax.fori_loop(taken % 8, 8, phase(taken // 8), acc)
+        for q in range(tiles):
+            af[m, 8 * q : 8 * q + 8, :] = acc[q]
 
     def component(c):
         each(0, 9, lambda b: coarse(c, b))
         each(0, 14, lambda b: fine(c, b))
         each(0, 17, lambda b: eights(c, b))
         scales(c)
-        for t0 in range(0, OUT, span):
-
-            def phase(f, acc):
-                win = [xt[c, pl.ds(t0 + f + 8 * q, 8), :] for q in range(tiles)]
-                for e in range(steps):
-                    h = jnp.broadcast_to(ht[c, pl.ds(f + 8 * e, 1), :], (8, LANES))
-                    acc = tuple(a + h * w for a, w in zip(acc, win))
-                    if e < steps - 1:
-                        win = win[1:] + [xt[c, pl.ds(t0 + f + 8 * (tiles + e), 8), :]]
-                return acc
-
-            acc = tuple(jnp.zeros((8, LANES), jnp.float32) for _ in range(tiles))
-            acc = lax.fori_loop(0, 8, phase, acc)
-            for tap in range(taps // 8 * 8, taps):
-                h = jnp.broadcast_to(ht[c, pl.ds(tap, 1), :], (8, LANES))
-                acc = tuple(
-                    a + h * xt[c, pl.ds(t0 + tap + 8 * q, 8), :] for q, a in enumerate(acc)
-                )
-            for q in range(tiles):
-                at = pl.ds(t0 + 8 * q, 8)
-                chan[at, :] += acc[q] * it[c, at, :]
+        each(0, 7, lambda b: parts(c, b))
+        each(0, 3, lambda m: correlate(c, m))
+        for q in range(tiles):
+            at = slice(8 * q, 8 * q + 8)
+            common = af[0, at, :]
+            even = it[c, pl.ds(16 * q, 8, stride=2), :]
+            odd = it[c, pl.ds(16 * q + 1, 8, stride=2), :]
+            chan[0, at, :] += (common + af[1, at, :]) * even
+            chan[1, at, :] += (common + af[2, at, :]) * odd
 
     each(0, 3, component)
-    flat = jnp.concatenate([chan[v : v + LANES].T for v in range(0, OUT, LANES)], axis=1)
+    for q in range(tiles):
+        line[pl.ds(16 * q, 8, stride=2), :] = chan[0, 8 * q : 8 * q + 8, :]
+        line[pl.ds(16 * q + 1, 8, stride=2), :] = chan[1, 8 * q : 8 * q + 8, :]
+    flat = jnp.concatenate([line[v : v + LANES, :].T for v in range(0, OUT, LANES)], axis=1)
     stack = jnp.concatenate(
         [jnp.sum(flat[k * nstat : (k + 1) * nstat], axis=0, keepdims=True) for k in range(sets)],
         axis=0,
@@ -264,7 +290,11 @@
             pltpu.VMEM((3, LANES, padded), jnp.float32),
             pltpu.VMEM((3, padded, LANES), jnp.float32),
             pltpu.VMEM((3, 8, LANES), jnp.float32),
+            pltpu.VMEM((3, 280, LANES), jnp.float32),
+            pltpu.VMEM((3, 3, padded // 2, LANES), jnp.float32),
+            pltpu.VMEM((3, OUT // 2, LANES), jnp.float32),
             pltpu.VMEM((OUT, LANES), jnp.float32),
+            pltpu.VMEM((2, OUT // 2, LANES), jnp.float32),
             pltpu.VMEM((1, OUT), jnp.float32),
             pltpu.VMEM((n, 1, OUT), jnp.float32),
             pltpu.SemaphoreType.DMA((5,)),

time: 34.7 us -> 32.2 us (0.928)
  Pallas kernels: 32 us -> 29.5 us
    pallas_call x1, Pallas kernels: 32 us -> 29.5 us  [on_device(): pl.pallas_call(functools.partial(kernel, n, stations, sets, nstat, taps),...]
where the time goes in v4:
time: 32.2 us; the launch traced here: 32 us
  Pallas kernels  29.5 us (92%)
  local copies, waits for them, and re-layouts  1.86 us (6%)
  between operations  0.65 us (2%)
    pallas_call x1, Pallas kernels, on_device(): pl.pallas_call(functools.partial(kernel, n, stations, sets, nstat, taps),...  29.5 us
    unnamed x4, local copies, waits for them, and re-layouts  1.86 us

profile of v4, /device:TPU:0, one launch (start us, length us, event | category | flops | bytes accessed | tf_op | source)
XLA Modules:
  0.0 32.0 jit_solution(6763271566994573580)
XLA Ops:
  0.6 29.5 %network_stack.1 = (f32[6,256]{1,0:T(8,128)}, f32[1,256]{1,0:T(1,128)}) custom-call(s32[2,16]{1,0:T(2,128)} %bitcast.10, s32[6,20]{1,0:T(8,128)} %slots_hbm.1, s32[6,20]{1,0:T(8,128)} %moves_hbm.1, bf16[48,768]{1,0:T(8,128)(2,1)} %bitcast.9, bf16[6,3,20,300]{3,2,1,0:T(8,128)(2,1)} %bitcast.8), custom_call_target="tpu_custom_call" | custom-call | tf_op jit(solution)/shard_map/network_stack/pallas_call | solution.py:266
  30.1 0.0 copy-start
  30.2 1.3 %copy.9 = f32[6,256]{1,0:T(8,128)} copy(f32[6,256]{1,0:T(8,128)} %get-tuple-element.8) | data formatting | bytes 12288
  31.4 0.0 copy-done
  31.5 0.6 %copy.10 = f32[256]{0:T(256)} copy(f32[256]{0:T(256)S(1)} %bitcast.11) | data formatting | bytes 2048
Async XLA Ops:
  30.1 1.3 %copy-start = (f32[1,256]{1,0:T(1,128)S(1)}, f32[1,256]{1,0:T(1,128)}, u32[]{:S(2)}) copy-start(f32[1,256]{1,0:T(1,128)} %get-tuple-element.5) | copy-start | bytes 3076

commit v5 on v4

--- a/solution.py
+++ b/solution.py
@@ -49,19 +49,15 @@
     moves_copy.start()
     tm_copy.start()
 
-    rx_ref[...] = jnp.zeros_like(rx_ref)
     barrier = pltpu.get_barrier_semaphore()
     each(1, n, lambda d: pl.semaphore_signal(
         barrier, inc=1, device_id={"tmpl": lax.rem(me + d, n)},
         device_id_type=pl.DeviceIdType.MESH))
 
-    row = lax.broadcasted_iota(jnp.int32, (8, LANES), 0)
-    comp = jnp.where(row < 3, row, row - 3)
+    lane = lax.broadcasted_iota(jnp.int32, (1, LANES), 1)
 
     def request(o):
-        wanted = jnp.where(row < 3, list_ref[0, o], list_ref[1, o])
-        valid = jnp.logical_and(wanted >= 0, row < 6)
-        req_ref[o] = jnp.where(valid, comp * stations + wanted, -1)
+        req_ref[o] = jnp.where(lane % 2 == 0, list_ref[0, o], list_ref[1, o])
 
     list_copy.wait()
     each(0, n, request)
@@ -71,9 +67,9 @@
         peer = lax.rem(me + d, n)
         return push(req_ref.at[peer], asked.at[me], s1.at[d], r1.at[d], peer)
 
-    def give(d):
+    def give(c, d):
         peer = lax.rem(me + d, n)
-        return push(stage.at[peer, pl.ds(0, 6)], rx_ref.at[me, pl.ds(0, 6)], s2.at[d], r2.at[d], peer)
+        return push(stage.at[c, peer], rx_ref.at[c, me], s2.at[c, d], r2.at[c, d], peer)
 
     def tell(d):
         peer = lax.rem(me + d, n)
@@ -106,29 +102,40 @@
 
     rec_copy.wait()
     each(1, n, lambda d: ask(d).wait())
-    rows = n * 8
-    depth, width = rec_ref.shape
-    want = asked[...].reshape(rows, LANES)[:, :depth]
-    spot = lax.broadcasted_iota(jnp.int32, (rows, depth), 1)
-    onehot = jnp.where(want == spot, 1.0, 0.0).astype(jnp.bfloat16)
-    picked = jnp.dot(onehot, rec_ref[...], preferred_element_type=jnp.float32)
-    stage[...] = picked.reshape(n, 8, width).astype(jnp.bfloat16)
-    each(1, n, lambda d: give(d).start())
-    rx_ref[me] = stage[me]
-
-    each(1, n, lambda d: give(d).wait())
-
-    spot = lax.broadcasted_iota(jnp.int32, (rows, LANES), 0)
-    slot = (ids[0:1, :] >> 1) * 8 + (ids[0:1, :] & 1) * 3
-    chosen = jnp.concatenate(
-        [jnp.where(spot == slot + c, 1.0, 0.0) for c in range(3)], axis=1
-    ).astype(jnp.bfloat16)
-    got = rx_ref[...].reshape(rows, width)
-    picked = lax.dot_general(
-        got, chosen, (((0,), (0,)), ((), ())), preferred_element_type=jnp.float32
-    )
+    width = rec_ref.shape[1]
+    slots = 2 * n
+    share = LANES // 2
+    asks = asked[...].reshape(n, LANES)
+    wants = []
+    for first in range(0, n, share):
+        some = asks[first : first + share]
+        holder = lax.broadcasted_iota(jnp.int32, some.shape, 0)
+        column = lax.broadcasted_iota(jnp.int32, some.shape, 1)
+        mine_here = jnp.where(column // 2 == holder, some, 0)
+        wants.append(jnp.sum(mine_here, axis=0, keepdims=True)[:, : 2 * some.shape[0]])
+    want = jnp.concatenate(wants, axis=1) if len(wants) > 1 else wants[0]
+    spot = lax.broadcasted_iota(jnp.int32, (stations, slots), 0)
+    onehot = jnp.where(spot == want, 1.0, 0.0).astype(jnp.bfloat16)
     for c in range(3):
-        xs[c, :width, :] = picked[:, c * LANES : (c + 1) * LANES]
+        picked = lax.dot_general(
+            onehot,
+            rec_ref[c * stations : (c + 1) * stations, :],
+            (((0,), (0,)), ((), ())),
+            preferred_element_type=jnp.float32,
+        )
+        stage[c] = picked.reshape(n, 2, width).astype(jnp.bfloat16)
+        each(1, n, functools.partial(lambda c, d: give(c, d).start(), c))
+        rx_ref[c, me] = stage[c, me]
+
+    spot = lax.broadcasted_iota(jnp.int32, (slots, LANES), 0)
+    chosen = jnp.where(spot == ids[0:1, :], 1.0, 0.0).astype(jnp.bfloat16)
+
+    def gather(c):
+        each(1, n, lambda d: give(c, d).wait())
+        got = rx_ref[c].astype(jnp.float32).reshape(slots, width).astype(jnp.bfloat16)
+        xs[c, :width, :] = lax.dot_general(
+            got, chosen, (((0,), (0,)), ((), ())), preferred_element_type=jnp.float32
+        )
 
     moves = jnp.broadcast_to(ids[8:9, :], (8, LANES))
     bits = {b: (moves & b) != 0 for b in (128, 64, 32, 16, 8, 4, 2, 1)}
@@ -219,6 +226,7 @@
             af[m, 8 * q : 8 * q + 8, :] = acc[q]
 
     def component(c):
+        gather(c)
         each(0, 9, lambda b: coarse(c, b))
         each(0, 14, lambda b: fine(c, b))
         each(0, 17, lambda b: eights(c, b))
@@ -262,6 +270,7 @@
     kernels = jnp.transpose(templates, (0, 2, 1, 3))
     vmem = pl.BlockSpec(memory_space=pltpu.VMEM)
     far = pl.BlockSpec(memory_space=pltpu.HBM)
+    many = pltpu.SemaphoreType.DMA((3, n))
     sems = pltpu.SemaphoreType.DMA((n,))
     stack, peak = pl.pallas_call(
         functools.partial(kernel, n, stations, sets, nstat, taps),
@@ -277,10 +286,10 @@
             pltpu.VMEM(moveouts.shape, jnp.int32),
             pltpu.VMEM(rec_flat.shape, jnp.bfloat16),
             pltpu.VMEM(kernels.shape, jnp.bfloat16),
-            pltpu.VMEM((n, 8, LANES), jnp.int32),
-            pltpu.VMEM((n, 8, LANES), jnp.int32),
-            pltpu.VMEM((n, 8, width), jnp.bfloat16),
-            pltpu.VMEM((n, 8, width), jnp.bfloat16),
+            pltpu.VMEM((n, 1, LANES), jnp.int32),
+            pltpu.VMEM((n, 1, LANES), jnp.int32),
+            pltpu.VMEM((3, n, 2, width), jnp.bfloat16),
+            pltpu.VMEM((3, n, 2, width), jnp.bfloat16),
             pltpu.VMEM((16, LANES), jnp.int32),
             pltpu.VMEM((3, 832, LANES), jnp.float32),
             pltpu.VMEM((576, LANES), jnp.float32),
@@ -298,7 +307,7 @@
             pltpu.VMEM((1, OUT), jnp.float32),
             pltpu.VMEM((n, 1, OUT), jnp.float32),
             pltpu.SemaphoreType.DMA((5,)),
-            sems, sems, sems, sems, sems, sems,
+            sems, sems, many, many, sems, sems,
         ],
         compiler_params=pltpu.CompilerParams(
             collective_id=0, has_side_effects=True, vmem_limit_bytes=60 << 20

time: 32.2 us -> 32.2 us (level)
  no operation moved by 1% of the time
where the time goes in v5:
time: 32.2 us; the launch traced here: 32.1 us
  Pallas kernels  29.5 us (92%)
  local copies, waits for them, and re-layouts  1.86 us (6%)
  between operations  0.65 us (2%)
    pallas_call x1, Pallas kernels, on_device(): pl.pallas_call(functools.partial(kernel, n, stations, sets, nstat, taps),...  29.5 us
    unnamed x4, local copies, waits for them, and re-layouts  1.86 us

profile of v5, /device:TPU:0, one launch (start us, length us, event | category | flops | bytes accessed | tf_op | source)
XLA Modules:
  0.0 32.1 jit_solution(1511028732169265996)
XLA Ops:
  0.6 29.5 %network_stack.1 = (f32[6,256]{1,0:T(8,128)}, f32[1,256]{1,0:T(1,128)}) custom-call(s32[2,16]{1,0:T(2,128)} %bitcast.10, s32[6,20]{1,0:T(8,128)} %slots_hbm.1, s32[6,20]{1,0:T(8,128)} %moves_hbm.1, bf16[48,768]{1,0:T(8,128)(2,1)} %bitcast.9, bf16[6,3,20,300]{3,2,1,0:T(8,128)(2,1)} %bitcast.8), custom_call_target="tpu_custom_call" | custom-call | tf_op jit(solution)/shard_map/network_stack/pallas_call | solution.py:275
  30.2 0.0 copy-start
  30.2 1.3 %copy.9 = f32[6,256]{1,0:T(8,128)} copy(f32[6,256]{1,0:T(8,128)} %get-tuple-element.8) | data formatting | bytes 12288
  31.5 0.0 copy-done
  31.5 0.6 %copy.10 = f32[256]{0:T(256)} copy(f32[256]{0:T(256)S(1)} %bitcast.11) | data formatting | bytes 2048
Async XLA Ops:
  30.2 1.3 %copy-start = (f32[1,256]{1,0:T(1,128)S(1)}, f32[1,256]{1,0:T(1,128)}, u32[]{:S(2)}) copy-start(f32[1,256]{1,0:T(1,128)} %get-tuple-element.5) | copy-start | bytes 3076

commit v6 on v5

--- a/solution.py
+++ b/solution.py
@@ -67,9 +67,10 @@
         peer = lax.rem(me + d, n)
         return push(req_ref.at[peer], asked.at[me], s1.at[d], r1.at[d], peer)
 
-    def give(c, d):
+    def give(m, d):
+        part = pl.ds(0, 1) if m == 0 else pl.ds(1, 2)
         peer = lax.rem(me + d, n)
-        return push(stage.at[c, peer], rx_ref.at[c, me], s2.at[c, d], r2.at[c, d], peer)
+        return push(stage.at[part, peer], rx_ref.at[part, me], s2.at[m, d], r2.at[m, d], peer)
 
     def tell(d):
         peer = lax.rem(me + d, n)
@@ -101,7 +102,7 @@
         tinv[c] = jnp.broadcast_to(1.0 / (taps * tscale), (8, LANES))
 
     rec_copy.wait()
-    each(1, n, lambda d: ask(d).wait())
+    each(1, n, lambda d: ask(d).wait_recv())
     width = rec_ref.shape[1]
     slots = 2 * n
     share = LANES // 2
@@ -124,14 +125,24 @@
             preferred_element_type=jnp.float32,
         )
         stage[c] = picked.reshape(n, 2, width).astype(jnp.bfloat16)
-        each(1, n, functools.partial(lambda c, d: give(c, d).start(), c))
+        if c == 0:
+            each(1, n, lambda d: give(0, d).start())
+        if c == 2:
+            each(1, n, lambda d: give(1, d).start())
         rx_ref[c, me] = stage[c, me]
 
     spot = lax.broadcasted_iota(jnp.int32, (slots, LANES), 0)
     chosen = jnp.where(spot == ids[0:1, :], 1.0, 0.0).astype(jnp.bfloat16)
 
     def gather(c):
-        each(1, n, lambda d: give(c, d).wait())
+        @pl.when(c == 0)
+        def _():
+            each(1, n, lambda d: give(0, d).wait_recv())
+
+        @pl.when(c == 1)
+        def _():
+            each(1, n, lambda d: give(1, d).wait_recv())
+
         got = rx_ref[c].astype(jnp.float32).reshape(slots, width).astype(jnp.bfloat16)
         xs[c, :width, :] = lax.dot_general(
             got, chosen, (((0,), (0,)), ((), ())), preferred_element_type=jnp.float32
@@ -255,8 +266,10 @@
     mine[...] = best
     each(1, n, lambda d: tell(d).start())
     held[me] = best
-    each(1, n, lambda d: tell(d).wait())
+    each(1, n, lambda d: tell(d).wait_recv())
     peak_ref[...] = jnp.max(held[...], axis=0)
+    for sent in (ask, functools.partial(give, 0), functools.partial(give, 1), tell):
+        each(1, n, functools.partial(lambda copy, d: copy(d).wait_send(), sent))
 
 
 def on_device(records, templates, fetch_list, cluster_slots, moveouts):
@@ -270,7 +283,7 @@
     kernels = jnp.transpose(templates, (0, 2, 1, 3))
     vmem = pl.BlockSpec(memory_space=pltpu.VMEM)
     far = pl.BlockSpec(memory_space=pltpu.HBM)
-    many = pltpu.SemaphoreType.DMA((3, n))
+    many = pltpu.SemaphoreType.DMA((2, n))
     sems = pltpu.SemaphoreType.DMA((n,))
     stack, peak = pl.pallas_call(
         functools.partial(kernel, n, stations, sets, nstat, taps),

time: 32.2 us -> 32.5 us (level)
  Pallas kernels: 29.5 us -> 29.9 us
where the time goes in v6:
time: 32.5 us; the launch traced here: 32.4 us
  Pallas kernels  29.9 us (92%)
  local copies, waits for them, and re-layouts  1.86 us (6%)
  between operations  0.65 us (2%)
    pallas_call x1, Pallas kernels, on_device(): pl.pallas_call(functools.partial(kernel, n, stations, sets, nstat, taps),...  29.9 us
    unnamed x4, local copies, waits for them, and re-layouts  1.86 us

profile of v6, /device:TPU:0, one launch (start us, length us, event | category | flops | bytes accessed | tf_op | source)
XLA Modules:
  0.0 32.4 jit_solution(2912021098423141433)
XLA Ops:
  0.6 29.9 %network_stack.1 = (f32[6,256]{1,0:T(8,128)}, f32[1,256]{1,0:T(1,128)}) custom-call(s32[2,16]{1,0:T(2,128)} %bitcast.10, s32[6,20]{1,0:T(8,128)} %slots_hbm.1, s32[6,20]{1,0:T(8,128)} %moves_hbm.1, bf16[48,768]{1,0:T(8,128)(2,1)} %bitcast.9, bf16[6,3,20,300]{3,2,1,0:T(8,128)(2,1)} %bitcast.8), custom_call_target="tpu_custom_call" | custom-call | tf_op jit(solution)/shard_map/network_stack/pallas_call | solution.py:288
  30.5 0.0 copy-start
  30.5 1.3 %copy.9 = f32[6,256]{1,0:T(8,128)} copy(f32[6,256]{1,0:T(8,128)} %get-tuple-element.8) | data formatting | bytes 12288
  31.8 0.0 copy-done
  31.8 0.6 %copy.10 = f32[256]{0:T(256)} copy(f32[256]{0:T(256)S(1)} %bitcast.11) | data formatting | bytes 2048
Async XLA Ops:
  30.5 1.3 %copy-start = (f32[1,256]{1,0:T(1,128)S(1)}, f32[1,256]{1,0:T(1,128)}, u32[]{:S(2)}) copy-start(f32[1,256]{1,0:T(1,128)} %get-tuple-element.5) | copy-start | bytes 3076
